TPU v7x, 32 devices: a whole 2x2x4 slice. The times are simulated.
32 devices in a mesh: blk: 8 (over y, x, core), rows: 4 (over z).
Axes of the slice: x: 2, y: 2, z: 4, core: 2. Of those that a mesh axis runs over, the one named last changes fastest.
Arguments:
- sens_tiles: bfloat16 [2048, 512, 128], P('blk', 'rows'), may hold values from -1 to 1
- start_basis: bfloat16 [64, 32768], P(None, 'blk'), may hold values from -6 to 6
- row_blocks: int32 [2048, 4], P('blk', 'rows'), may hold values from 0 to 7, as said below
- col_blocks: int32 [2048, 4], P('blk', 'rows'), may hold values from 0 to 31, as said below
- live_counts: int32 [8, 4], P('blk', 'rows'), may hold values from 64 to 256, as said below
Outputs:
- orthonormal: float32 [4, 64, 32768], P(None, None, ('blk', 'rows'))
Inputs may be any that keep to these rules, and one draw needn't show every extreme that they name: Within one device the pairs (row_blocks, col_blocks) of its 256 slots are distinct. Within one device the pairs (row_blocks, col_blocks) of its 256 slots are distinct. Slots 0 to live_counts - 1 of a device hold its tiles; some device has all 256 slots live.
All inputs are finite; a program needn't handle non-finite values.
Results may differ from a plain program's by a relative error of at most 0.012.
The roundings to bfloat16 on the way count: a program that leaves them out, or rounds other values in their place, can miss the bound.
Values may be sent and summed in bfloat16 or wider, within the bound.
A program may use at most 128 MiB of HBM per device.

v0:
```python
import jax
import jax.numpy as jnp
from jax import lax
from jax.sharding import PartitionSpec as P

RB = 8
CB = 32
ITERS = 4


def apply_forward(sens_tiles, basis_now, col_slots, row_onehot):
    vectors = basis_now.shape[0]
    tile_size = sens_tiles.shape[2]
    picked = jnp.take(basis_now.reshape(vectors, CB, tile_size), col_slots, axis=1)
    products = jnp.einsum("kst,sit->ksi", picked, sens_tiles, preferred_element_type=jnp.float32)
    summed = jnp.einsum("ksi,rs->kri", products, row_onehot, precision=lax.Precision.HIGHEST)
    return summed.reshape(vectors, RB * tile_size)


def apply_backward(sens_tiles, image_half, row_slots, col_onehot):
    vectors = image_half.shape[0]
    tile_size = sens_tiles.shape[2]
    picked = jnp.take(image_half.reshape(vectors, RB, tile_size), row_slots, axis=1)
    products = jnp.einsum("ksi,sij->ksj", picked, sens_tiles, preferred_element_type=jnp.float32)
    summed = jnp.einsum("ksj,cs->kcj", products, col_onehot, precision=lax.Precision.HIGHEST)
    return summed.reshape(vectors, CB * tile_size)


def factor_whole(current, total):
    local_gram = jnp.dot(current, current.T, precision=lax.Precision.HIGHEST)
    gram = lax.psum(local_gram, "blk") / total
    lower = jnp.linalg.cholesky(gram)
    return jax.scipy.linalg.solve_triangular(lower, current, lower=True)


def local(sens_tiles, start_basis, row_blocks, col_blocks, live_counts):
    row_slots = row_blocks[:, 0]
    col_slots = col_blocks[:, 0]
    count_live = live_counts[0, 0]
    slot_total = sens_tiles.shape[0]
    tile_size = sens_tiles.shape[2]
    live = jnp.arange(slot_total) < count_live
    row_onehot = ((row_slots[None, :] == jnp.arange(RB)[:, None]) & live[None, :]).astype(
        jnp.float32
    )
    col_onehot = ((col_slots[None, :] == jnp.arange(CB)[:, None]) & live[None, :]).astype(
        jnp.float32
    )
    total = float(CB * tile_size * lax.axis_size("blk"))
    own_width = CB * tile_size // lax.axis_size("rows")
    basis_now = start_basis
    results = []
    for iteration in range(ITERS):
        partial_image = apply_forward(sens_tiles, basis_now, col_slots, row_onehot)
        image = lax.psum(partial_image, "blk")
        image_half = image.astype(jnp.bfloat16)
        partial_hessian = apply_backward(sens_tiles, image_half, row_slots, col_onehot)
        hessian = lax.psum(partial_hessian, "rows")
        whole_result = factor_whole(hessian, total)
        basis_now = whole_result.astype(jnp.bfloat16)
        result = lax.dynamic_slice_in_dim(
            whole_result, lax.axis_index("rows") * own_width, own_width, 1
        )
        results.append(result)
    return jnp.stack(results, axis=0)


def solution(mesh):
    in_specs = (
        P("blk", "rows", None),
        P(None, "blk"),
        P("blk", "rows"),
        P("blk", "rows"),
        P("blk", "rows"),
    )
    out_specs = P(None, None, ("blk", "rows"))
    return jax.shard_map(local, mesh=mesh, in_specs=in_specs, out_specs=out_specs, check_vma=False)
```

profile of v0, /device:TPU:0, one launch (start us, length us, event | category | flops | bytes accessed | tf_op | source)
XLA Modules:
  0.0 653.3 jit_solution(9419659961309902612)
XLA Ops:
  12.5 10.4 %fusion.48 = f32[64,256,128]{2,0,1:T(8,128)S(1)} fusion(bf16[256,128,128]{2,1,0:T(8,128)(2,1)} %param.12, bf16[256,64,128]{2,1,0:T(8,128)(2,1)} %gather_fusion, pred[256]{0:T(512)(128)(4,1)S(1)} %get-tuple-element.8), kind=kOutput, calls=%fused_computation.56 | convolution fusion | flops 538968064 | bytes 20971776 | tf_op jit(solution)/shard_map/kst,sit->ksi/dot_general | solution.py:15
  22.9 7.5 %fusion.14 = f32[8,64,128]{2,0,1:T(8,128)S(1)} fusion(f32[64,256,128]{2,0,1:T(8,128)S(1)} %fusion.48, s32[256]{0:T(256)S(1)} %bitcast.242, pred[256]{0:T(512)(128)(4,1)S(1)} %iota_compare_fusion.4), kind=kOutput, calls=%fused_computation.22 | convolution fusion | flops 201330688 | bytes 8652032 | tf_op jit(solution)/shard_map/ksi,rs->kri/dot_general | solution.py:16
  30.8 28.4 %all-reduce.16 = bf16[64,1024]{1,0:T(8,128)(2,1)S(1)} all-reduce(f32[64,1024]{1,0:T(8,128)S(1)} %bitcast.236), channel_id=1, replica_groups=mesh['blk'=8,'rows'=4] {'blk'}, use_global_device_ids=true, to_apply=%region_0.0 | all-reduce | flops 65536 | bytes 393216 | tf_op jit(solution)/shard_map/psum | solution.py:55
  69.4 7.7 %fusion.12 = f32[32,64,128]{2,0,1:T(8,128)S(1)} fusion(f32[64,256,128]{2,0,1:T(8,128)S(1)} %fusion.51, s32[256]{0:T(256)S(1)} %bitcast.248, pred[256]{0:T(512)(128)(4,1)S(1)} %iota_compare_fusion.4), kind=kOutput, calls=%fused_computation.20 | convolution fusion | flops 805322752 | bytes 9438464 | tf_op jit(solution)/shard_map/ksj,cs->kcj/dot_general | solution.py:25
  78.7 51.6 %all-reduce.9.cloned.1.call-done = f32[64,4096]{1,0:T(8,128)} async-done(((f32[64,4096]{1,0:T(8,128)}), f32[64,4096]{1,0:T(8,128)}) %all-reduce.9.cloned.1.call-update) | async-done | bytes 1048592 | tf_op jit(solution)/shard_map/psum | solution.py:58
  132.8 24.3 %psum.86 = f32[64,64]{0,1:T(8,128)S(1)} all-reduce(f32[64,64]{0,1:T(8,128)S(1)} %fusion.116), channel_id=1, replica_groups=mesh['blk'=8,'rows'=4] {'blk'}, use_global_device_ids=true, to_apply=%region_2.0 | all-reduce | flops 4096 | bytes 32768 | tf_op jit(solution)/shard_map/psum | solution.py:31
  175.7 10.4 %fusion.54 = f32[64,256,128]{2,0,1:T(8,128)S(1)} fusion(bf16[256,128,128]{2,1,0:T(8,128)(2,1)} %param.12, bf16[256,64,128]{2,1,0:T(8,128)(2,1)} %gather_fusion.2, pred[256]{0:T(512)(128)(4,1)S(1)} %get-tuple-element.8), kind=kOutput, calls=%fused_computation.58 | convolution fusion | flops 538968064 | bytes 20971776 | tf_op jit(solution)/shard_map/kst,sit->ksi/dot_general | solution.py:15
  186.1 7.9 %fusion.10 = f32[8,64,128]{2,0,1:T(8,128)S(1)} fusion(f32[64,256,128]{2,0,1:T(8,128)S(1)} %fusion.54, s32[256]{0:T(256)S(1)} %bitcast.243, pred[256]{0:T(512)(128)(4,1)S(1)} %iota_compare_fusion.4), kind=kOutput, calls=%fused_computation.18 | convolution fusion | flops 201330688 | bytes 8652032 | tf_op jit(solution)/shard_map/ksi,rs->kri/dot_general | solution.py:16
  194.0 25.3 %all-reduce.17 = bf16[64,1024]{1,0:T(8,128)(2,1)S(1)} all-reduce(f32[64,1024]{1,0:T(8,128)S(1)} %bitcast.237), channel_id=1, replica_groups=mesh['blk'=8,'rows'=4] {'blk'}, use_global_device_ids=true, to_apply=%region_5.10 | all-reduce | flops 65536 | bytes 393216 | tf_op jit(solution)/shard_map/psum | solution.py:55
  229.4 7.7 %fusion.8 = f32[32,64,128]{2,0,1:T(8,128)S(1)} fusion(f32[64,256,128]{2,0,1:T(8,128)S(1)} %fusion.57, s32[256]{0:T(256)S(1)} %bitcast.249, pred[256]{0:T(512)(128)(4,1)S(1)} %iota_compare_fusion.4), kind=kOutput, calls=%fused_computation.16 | convolution fusion | flops 805322752 | bytes 9438464 | tf_op jit(solution)/shard_map/ksj,cs->kcj/dot_general | solution.py:25
  238.8 49.5 %all-reduce.11.cloned.1.call-done = f32[64,4096]{1,0:T(8,128)} async-done(((f32[64,4096]{1,0:T(8,128)}), f32[64,4096]{1,0:T(8,128)}) %all-reduce.11.cloned.1.call-update) | async-done | bytes 1048592 | tf_op jit(solution)/shard_map/psum | solution.py:58
  290.7 24.3 %psum.89 = f32[64,64]{0,1:T(8,128)S(1)} all-reduce(f32[64,64]{0,1:T(8,128)S(1)} %fusion.117), channel_id=1, replica_groups=mesh['blk'=8,'rows'=4] {'blk'}, use_global_device_ids=true, to_apply=%region_7.12 | all-reduce | flops 4096 | bytes 32768 | tf_op jit(solution)/shard_map/psum | solution.py:31
  333.6 10.4 %fusion.60 = f32[64,256,128]{2,0,1:T(8,128)S(1)} fusion(bf16[256,128,128]{2,1,0:T(8,128)(2,1)} %param.12, bf16[256,64,128]{2,1,0:T(8,128)(2,1)} %gather_fusion.4, pred[256]{0:T(512)(128)(4,1)S(1)} %get-tuple-element.8), kind=kOutput, calls=%fused_computation.60 | convolution fusion | flops 538968064 | bytes 20971776 | tf_op jit(solution)/shard_map/kst,sit->ksi/dot_general | solution.py:15
  344.0 7.9 %fusion.6 = f32[8,64,128]{2,0,1:T(8,128)S(1)} fusion(f32[64,256,128]{2,0,1:T(8,128)S(1)} %fusion.60, s32[256]{0:T(256)S(1)} %bitcast.244, pred[256]{0:T(512)(128)(4,1)S(1)} %iota_compare_fusion.4), kind=kOutput, calls=%fused_computation.14 | convolution fusion | flops 201330688 | bytes 8652032 | tf_op jit(solution)/shard_map/ksi,rs->kri/dot_general | solution.py:16
  352.0 25.3 %all-reduce.18 = bf16[64,1024]{1,0:T(8,128)(2,1)S(1)} all-reduce(f32[64,1024]{1,0:T(8,128)S(1)} %bitcast.238), channel_id=1, replica_groups=mesh['blk'=8,'rows'=4] {'blk'}, use_global_device_ids=true, to_apply=%region_8.13 | all-reduce | flops 65536 | bytes 393216 | tf_op jit(solution)/shard_map/psum | solution.py:55
  387.3 7.7 %fusion.4 = f32[32,64,128]{2,0,1:T(8,128)S(1)} fusion(f32[64,256,128]{2,0,1:T(8,128)S(1)} %fusion.63, s32[256]{0:T(256)S(1)} %bitcast.250, pred[256]{0:T(512)(128)(4,1)S(1)} %iota_compare_fusion.4), kind=kOutput, calls=%fused_computation.12 | convolution fusion | flops 805322752 | bytes 9438464 | tf_op jit(solution)/shard_map/ksj,cs->kcj/dot_general | solution.py:25
  396.7 49.5 %all-reduce.13.cloned.1.call-done = f32[64,4096]{1,0:T(8,128)} async-done(((f32[64,4096]{1,0:T(8,128)}), f32[64,4096]{1,0:T(8,128)}) %all-reduce.13.cloned.1.call-update) | async-done | bytes 1048592 | tf_op jit(solution)/shard_map/psum | solution.py:58
  448.7 24.2 %psum.92 = f32[64,64]{0,1:T(8,128)S(1)} all-reduce(f32[64,64]{0,1:T(8,128)S(1)} %fusion.118), channel_id=1, replica_groups=mesh['blk'=8,'rows'=4] {'blk'}, use_global_device_ids=true, to_apply=%region_10.15 | all-reduce | flops 4096 | bytes 32768 | tf_op jit(solution)/shard_map/psum | solution.py:31
  491.6 10.4 %fusion.66 = f32[64,256,128]{2,0,1:T(8,128)S(1)} fusion(bf16[256,128,128]{2,1,0:T(8,128)(2,1)} %param.12, bf16[256,64,128]{2,1,0:T(8,128)(2,1)} %gather_fusion.6, pred[256]{0:T(512)(128)(4,1)S(1)} %get-tuple-element.8), kind=kOutput, calls=%fused_computation.62 | convolution fusion | flops 538968064 | bytes 20971776 | tf_op jit(solution)/shard_map/kst,sit->ksi/dot_general | solution.py:15
  501.9 7.7 %fusion.2 = f32[8,64,128]{2,0,1:T(8,128)S(1)} fusion(f32[64,256,128]{2,0,1:T(8,128)S(1)} %fusion.66, s32[256]{0:T(256)S(1)} %bitcast.245, pred[256]{0:T(512)(128)(4,1)S(1)} %iota_compare_fusion.4), kind=kOutput, calls=%fused_computation.10 | convolution fusion | flops 201330688 | bytes 8652032 | tf_op jit(solution)/shard_map/ksi,rs->kri/dot_general | solution.py:16
  509.7 25.3 %all-reduce.19 = bf16[64,1024]{1,0:T(8,128)(2,1)S(1)} all-reduce(f32[64,1024]{1,0:T(8,128)S(1)} %bitcast.239), channel_id=1, replica_groups=mesh['blk'=8,'rows'=4] {'blk'}, use_global_device_ids=true, to_apply=%region_11.16 | all-reduce | flops 65536 | bytes 393216 | tf_op jit(solution)/shard_map/psum | solution.py:55
  545.1 7.7 %fusion = f32[32,64,128]{2,0,1:T(8,128)S(1)} fusion(f32[64,256,128]{2,0,1:T(8,128)S(1)} %fusion.69, s32[256]{0:T(256)S(1)} %bitcast.251, pred[256]{0:T(512)(128)(4,1)S(1)} %iota_compare_fusion.4), kind=kOutput, calls=%fused_computation.8 | convolution fusion | flops 805322752 | bytes 9438464 | tf_op jit(solution)/shard_map/ksj,cs->kcj/dot_general | solution.py:25
  557.4 46.5 %all-reduce.15.cloned.1.call-done = f32[64,4096]{1,0:T(8,128)} async-done(((f32[64,4096]{1,0:T(8,128)}), f32[64,4096]{1,0:T(8,128)}) %all-reduce.15.cloned.1.call-update) | async-done | bytes 1048592 | tf_op jit(solution)/shard_map/psum | solution.py:58
  606.7 24.1 %psum.95 = f32[64,64]{0,1:T(8,128)S(1)} all-reduce(f32[64,64]{0,1:T(8,128)S(1)} %fusion.119), channel_id=1, replica_groups=mesh['blk'=8,'rows'=4] {'blk'}, use_global_device_ids=true, to_apply=%region_13.18 | all-reduce | flops 4096 | bytes 32768 | tf_op jit(solution)/shard_map/psum | solution.py:31
  (101 shorter events, 137.2 us)
Async XLA Ops:
  6.5 2.8 copy-start
  6.5 123.8 %all-reduce.9.cloned.1.call-start = ((), (), s32[]{:S(2)}) async-start(), calls=%async_computation | async-start | bytes 2097152 | tf_op jit(solution)/shard_map/psum | solution.py:58
  12.5 10.4 %copy-start.5 = (s32[256,1]{0,1:T(1,128)S(1)}, s32[256,1]{0,1:T(1,128)}, u32[]{:S(2)}) copy-start(s32[256,1]{0,1:T(1,128)} %param.14) | copy-start | bytes 3076
  62.3 7.0 %copy-start.6 = (s32[256,1]{0,1:T(1,128)S(1)}, s32[256,1]{0,1:T(1,128)}, u32[]{:S(2)}) copy-start(s32[256,1]{0,1:T(1,128)} %param.15) | copy-start | bytes 3076
  78.7 209.5 %all-reduce.11.cloned.1.call-start = ((), (), s32[]{:S(2)}) async-start(), calls=%async_computation.1 | async-start | bytes 2097152 | tf_op jit(solution)/shard_map/psum | solution.py:58
  171.6 1.0 copy-start.2
  238.7 207.5 %all-reduce.13.cloned.1.call-start = ((), (), s32[]{:S(2)}) async-start(), calls=%async_computation.2 | async-start | bytes 2097152 | tf_op jit(solution)/shard_map/psum | solution.py:58
  329.5 1.0 copy-start.3
  396.7 207.2 %all-reduce.15.cloned.1.call-start = ((), (), s32[]{:S(2)}) async-start(), calls=%async_computation.3 | async-start | bytes 2097152 | tf_op jit(solution)/shard_map/psum | solution.py:58
  487.4 1.0 copy-start.4
  554.4 91.9 %copy-start.1 = (bf16[64,4096]{1,0:T(8,128)(2,1)S(1)}, bf16[64,4096]{1,0:T(8,128)(2,1)}, u32[]{:S(2)}) copy-start(bf16[64,4096]{1,0:T(8,128)(2,1)} %param.13) | copy-start | bytes 1572868
Sparse Core Ops, SparseCore 0:
  78.8 51.4 all-reduce.8
  238.8 49.3 all-reduce.10
  396.8 49.3 all-reduce.12
  554.5 49.3 all-reduce.14
where the time goes:
time: 663 us; the launch traced here: 653 us
  blocking collectives  201 us (30%)
  waiting for transfers between devices  197 us (30%)
  matrix products  151 us (23%)
  other arithmetic  51.9 us (8%)
  local copies, waits for them, and re-layouts  37.5 us (6%)
  between operations  14.7 us (2%)
    psum x4, waiting for transfers between devices, local(): hessian = lax.psum(partial_hessian, 'rows')  197 us
    psum x4, blocking collectives, local(): image = lax.psum(partial_image, 'blk')  104 us
    psum x4, blocking collectives, factor_whole(): gram = lax.psum(local_gram, 'blk') / total  96.9 us
    dot_general x4, matrix products, apply_forward(): jnp.einsum('kst,sit->ksi', picked, sens_tiles, preferred_element_type=jnp...  41.5 us
    dot_general x4, matrix products, apply_forward(): jnp.einsum('ksi,rs->kri', products, row_onehot, precision=lax.Precision.H...  31 us
    dot_general x4, matrix products, apply_backward(): jnp.einsum('ksj,cs->kcj', products, col_onehot, precision=lax.Precision.H...  30.9 us
    dot_general x4, matrix products, apply_backward(): jnp.einsum('ksi,sij->ksj', picked, sens_tiles, preferred_element_type=jnp...  28.1 us
    another operation x12, other arithmetic, factor_whole(): lower = jnp.linalg.cholesky(gram)  26.1 us
  transfers between devices with their start and end apart: 4, of which 4 were waited for; matrix products, arithmetic and copies ran while one was open for 0% of the time, Pallas kernels for 0%

commit v1 on v0

--- a/solution.py
+++ b/solution.py
@@ -28,7 +28,7 @@
 
 def factor_whole(current, total):
     local_gram = jnp.dot(current, current.T, precision=lax.Precision.HIGHEST)
-    gram = lax.psum(local_gram, "blk") / total
+    gram = jax.lax.all_gather(local_gram, "blk").sum(axis=0) / total
     lower = jnp.linalg.cholesky(gram)
     return jax.scipy.linalg.solve_triangular(lower, current, lower=True)
 

time: 663 us -> 610 us (0.920)
  blocking collectives: 201 us -> 145 us
    psum x4 -> x0, blocking collectives: 96.9 us -> none  [factor_whole(): gram = lax.psum(local_gram, 'blk') / total]
    all_gather x0 -> x4, blocking collectives: none -> 37.6 us  [factor_whole(): gram = jax.lax.all_gather(local_gram, 'blk').sum(axis=0) / total]
where the time goes in v1:
time: 610 us; the launch traced here: 601 us
  waiting for transfers between devices  200 us (33%)
  matrix products  151 us (25%)
  blocking collectives  145 us (24%)
  other arithmetic  52 us (9%)
  local copies, waits for them, and re-layouts  37.8 us (6%)
  between operations  14.7 us (2%)
    psum x4, waiting for transfers between devices, local(): hessian = lax.psum(partial_hessian, 'rows')  200 us
    psum x4, blocking collectives, local(): image = lax.psum(partial_image, 'blk')  108 us
    dot_general x4, matrix products, apply_forward(): jnp.einsum('kst,sit->ksi', picked, sens_tiles, preferred_element_type=jnp...  41.5 us
    all_gather x4, blocking collectives, factor_whole(): gram = jax.lax.all_gather(local_gram, 'blk').sum(axis=0) / total  37.6 us
    dot_general x4, matrix products, apply_forward(): jnp.einsum('ksi,rs->kri', products, row_onehot, precision=lax.Precision.H...  31 us
    dot_general x4, matrix products, apply_backward(): jnp.einsum('ksj,cs->kcj', products, col_onehot, precision=lax.Precision.H...  30.9 us
    dot_general x4, matrix products, apply_backward(): jnp.einsum('ksi,sij->ksj', picked, sens_tiles, preferred_element_type=jnp...  28.1 us
    another operation x12, other arithmetic, factor_whole(): lower = jnp.linalg.cholesky(gram)  26.1 us
  transfers between devices with their start and end apart: 4, of which 4 were waited for; matrix products, arithmetic and copies ran while one was open for 0% of the time, Pallas kernels for 0%

profile of v1, /device:TPU:0, one launch (start us, length us, event | category | flops | bytes accessed | tf_op | source)
XLA Modules:
  0.0 600.6 jit_solution(15761520218252803862)
XLA Ops:
  12.5 10.4 %fusion.48 = f32[64,256,128]{2,0,1:T(8,128)S(1)} fusion(bf16[256,128,128]{2,1,0:T(8,128)(2,1)} %param.12, bf16[256,64,128]{2,1,0:T(8,128)(2,1)} %gather_fusion, pred[256]{0:T(512)(128)(4,1)S(1)} %get-tuple-element.8), kind=kOutput, calls=%fused_computation.56 | convolution fusion | flops 538968064 | bytes 20971776 | tf_op jit(solution)/shard_map/kst,sit->ksi/dot_general | solution.py:15
  22.9 7.5 %fusion.14 = f32[8,64,128]{2,0,1:T(8,128)S(1)} fusion(f32[64,256,128]{2,0,1:T(8,128)S(1)} %fusion.48, s32[256]{0:T(256)S(1)} %bitcast.250, pred[256]{0:T(512)(128)(4,1)S(1)} %iota_compare_fusion.4), kind=kOutput, calls=%fused_computation.22 | convolution fusion | flops 201330688 | bytes 8652032 | tf_op jit(solution)/shard_map/ksi,rs->kri/dot_general | solution.py:16
  30.8 28.4 %all-reduce.16 = bf16[64,1024]{1,0:T(8,128)(2,1)S(1)} all-reduce(f32[64,1024]{1,0:T(8,128)S(1)} %bitcast.244), channel_id=1, replica_groups=mesh['blk'=8,'rows'=4] {'blk'}, use_global_device_ids=true, to_apply=%region_0.0 | all-reduce | flops 65536 | bytes 393216 | tf_op jit(solution)/shard_map/psum | solution.py:55
  69.4 7.7 %fusion.12 = f32[32,64,128]{2,0,1:T(8,128)S(1)} fusion(f32[64,256,128]{2,0,1:T(8,128)S(1)} %fusion.51, s32[256]{0:T(256)S(1)} %bitcast.256, pred[256]{0:T(512)(128)(4,1)S(1)} %iota_compare_fusion.4), kind=kOutput, calls=%fused_computation.20 | convolution fusion | flops 805322752 | bytes 9438464 | tf_op jit(solution)/shard_map/ksj,cs->kcj/dot_general | solution.py:25
  78.7 51.6 %all-reduce.9.cloned.1.call-done = f32[64,4096]{1,0:T(8,128)} async-done(((f32[64,4096]{1,0:T(8,128)}), f32[64,4096]{1,0:T(8,128)}) %all-reduce.9.cloned.1.call-update) | async-done | bytes 1048592 | tf_op jit(solution)/shard_map/psum | solution.py:58
  132.8 9.4 %all-gather = f32[512,64]{1,0:T(8,128)S(1)} all-gather(f32[64,64]{1,0:T(8,128)S(1)} %fusion.116), channel_id=2, replica_groups=mesh['blk'=8,'rows'=4] {'blk'}, dimensions={0}, use_global_device_ids=true | all-gather | bytes 147456 | tf_op jit(solution)/shard_map/all_gather | solution.py:31
  161.0 10.4 %fusion.54 = f32[64,256,128]{2,0,1:T(8,128)S(1)} fusion(bf16[256,128,128]{2,1,0:T(8,128)(2,1)} %param.12, bf16[256,64,128]{2,1,0:T(8,128)(2,1)} %gather_fusion.2, pred[256]{0:T(512)(128)(4,1)S(1)} %get-tuple-element.8), kind=kOutput, calls=%fused_computation.58 | convolution fusion | flops 538968064 | bytes 20971776 | tf_op jit(solution)/shard_map/kst,sit->ksi/dot_general | solution.py:15
  171.3 7.9 %fusion.10 = f32[8,64,128]{2,0,1:T(8,128)S(1)} fusion(f32[64,256,128]{2,0,1:T(8,128)S(1)} %fusion.54, s32[256]{0:T(256)S(1)} %bitcast.251, pred[256]{0:T(512)(128)(4,1)S(1)} %iota_compare_fusion.4), kind=kOutput, calls=%fused_computation.18 | convolution fusion | flops 201330688 | bytes 8652032 | tf_op jit(solution)/shard_map/ksi,rs->kri/dot_general | solution.py:16
  179.3 26.4 %all-reduce.17 = bf16[64,1024]{1,0:T(8,128)(2,1)S(1)} all-reduce(f32[64,1024]{1,0:T(8,128)S(1)} %bitcast.245), channel_id=1, replica_groups=mesh['blk'=8,'rows'=4] {'blk'}, use_global_device_ids=true, to_apply=%region_5.10 | all-reduce | flops 65536 | bytes 393216 | tf_op jit(solution)/shard_map/psum | solution.py:55
  215.8 7.7 %fusion.8 = f32[32,64,128]{2,0,1:T(8,128)S(1)} fusion(f32[64,256,128]{2,0,1:T(8,128)S(1)} %fusion.57, s32[256]{0:T(256)S(1)} %bitcast.257, pred[256]{0:T(512)(128)(4,1)S(1)} %iota_compare_fusion.4), kind=kOutput, calls=%fused_computation.16 | convolution fusion | flops 805322752 | bytes 9438464 | tf_op jit(solution)/shard_map/ksj,cs->kcj/dot_general | solution.py:25
  225.2 50.4 %all-reduce.11.cloned.1.call-done = f32[64,4096]{1,0:T(8,128)} async-done(((f32[64,4096]{1,0:T(8,128)}), f32[64,4096]{1,0:T(8,128)}) %all-reduce.11.cloned.1.call-update) | async-done | bytes 1048592 | tf_op jit(solution)/shard_map/psum | solution.py:58
  278.1 9.4 %all-gather.1 = f32[512,64]{1,0:T(8,128)S(1)} all-gather(f32[64,64]{1,0:T(8,128)S(1)} %fusion.117), channel_id=3, replica_groups=mesh['blk'=8,'rows'=4] {'blk'}, dimensions={0}, use_global_device_ids=true | all-gather | bytes 147456 | tf_op jit(solution)/shard_map/all_gather | solution.py:31
  306.3 10.4 %fusion.60 = f32[64,256,128]{2,0,1:T(8,128)S(1)} fusion(bf16[256,128,128]{2,1,0:T(8,128)(2,1)} %param.12, bf16[256,64,128]{2,1,0:T(8,128)(2,1)} %gather_fusion.4, pred[256]{0:T(512)(128)(4,1)S(1)} %get-tuple-element.8), kind=kOutput, calls=%fused_computation.60 | convolution fusion | flops 538968064 | bytes 20971776 | tf_op jit(solution)/shard_map/kst,sit->ksi/dot_general | solution.py:15
  316.6 7.9 %fusion.6 = f32[8,64,128]{2,0,1:T(8,128)S(1)} fusion(f32[64,256,128]{2,0,1:T(8,128)S(1)} %fusion.60, s32[256]{0:T(256)S(1)} %bitcast.252, pred[256]{0:T(512)(128)(4,1)S(1)} %iota_compare_fusion.4), kind=kOutput, calls=%fused_computation.14 | convolution fusion | flops 201330688 | bytes 8652032 | tf_op jit(solution)/shard_map/ksi,rs->kri/dot_general | solution.py:16
  324.6 26.4 %all-reduce.18 = bf16[64,1024]{1,0:T(8,128)(2,1)S(1)} all-reduce(f32[64,1024]{1,0:T(8,128)S(1)} %bitcast.246), channel_id=1, replica_groups=mesh['blk'=8,'rows'=4] {'blk'}, use_global_device_ids=true, to_apply=%region_8.13 | all-reduce | flops 65536 | bytes 393216 | tf_op jit(solution)/shard_map/psum | solution.py:55
  361.1 7.7 %fusion.4 = f32[32,64,128]{2,0,1:T(8,128)S(1)} fusion(f32[64,256,128]{2,0,1:T(8,128)S(1)} %fusion.63, s32[256]{0:T(256)S(1)} %bitcast.258, pred[256]{0:T(512)(128)(4,1)S(1)} %iota_compare_fusion.4), kind=kOutput, calls=%fused_computation.12 | convolution fusion | flops 805322752 | bytes 9438464 | tf_op jit(solution)/shard_map/ksj,cs->kcj/dot_general | solution.py:25
  370.5 50.3 %all-reduce.13.cloned.1.call-done = f32[64,4096]{1,0:T(8,128)} async-done(((f32[64,4096]{1,0:T(8,128)}), f32[64,4096]{1,0:T(8,128)}) %all-reduce.13.cloned.1.call-update) | async-done | bytes 1048592 | tf_op jit(solution)/shard_map/psum | solution.py:58
  423.4 9.4 %all-gather.2 = f32[512,64]{1,0:T(8,128)S(1)} all-gather(f32[64,64]{1,0:T(8,128)S(1)} %fusion.118), channel_id=4, replica_groups=mesh['blk'=8,'rows'=4] {'blk'}, dimensions={0}, use_global_device_ids=true | all-gather | bytes 147456 | tf_op jit(solution)/shard_map/all_gather | solution.py:31
  451.5 10.4 %fusion.66 = f32[64,256,128]{2,0,1:T(8,128)S(1)} fusion(bf16[256,128,128]{2,1,0:T(8,128)(2,1)} %param.12, bf16[256,64,128]{2,1,0:T(8,128)(2,1)} %gather_fusion.6, pred[256]{0:T(512)(128)(4,1)S(1)} %get-tuple-element.8), kind=kOutput, calls=%fused_computation.62 | convolution fusion | flops 538968064 | bytes 20971776 | tf_op jit(solution)/shard_map/kst,sit->ksi/dot_general | solution.py:15
  461.9 7.7 %fusion.2 = f32[8,64,128]{2,0,1:T(8,128)S(1)} fusion(f32[64,256,128]{2,0,1:T(8,128)S(1)} %fusion.66, s32[256]{0:T(256)S(1)} %bitcast.253, pred[256]{0:T(512)(128)(4,1)S(1)} %iota_compare_fusion.4), kind=kOutput, calls=%fused_computation.10 | convolution fusion | flops 201330688 | bytes 8652032 | tf_op jit(solution)/shard_map/ksi,rs->kri/dot_general | solution.py:16
  469.7 26.4 %all-reduce.19 = bf16[64,1024]{1,0:T(8,128)(2,1)S(1)} all-reduce(f32[64,1024]{1,0:T(8,128)S(1)} %bitcast.247), channel_id=1, replica_groups=mesh['blk'=8,'rows'=4] {'blk'}, use_global_device_ids=true, to_apply=%region_11.16 | all-reduce | flops 65536 | bytes 393216 | tf_op jit(solution)/shard_map/psum | solution.py:55
  506.2 7.7 %fusion = f32[32,64,128]{2,0,1:T(8,128)S(1)} fusion(f32[64,256,128]{2,0,1:T(8,128)S(1)} %fusion.69, s32[256]{0:T(256)S(1)} %bitcast.259, pred[256]{0:T(512)(128)(4,1)S(1)} %iota_compare_fusion.4), kind=kOutput, calls=%fused_computation.8 | convolution fusion | flops 805322752 | bytes 9438464 | tf_op jit(solution)/shard_map/ksj,cs->kcj/dot_general | solution.py:25
  518.5 47.4 %all-reduce.15.cloned.1.call-done = f32[64,4096]{1,0:T(8,128)} async-done(((f32[64,4096]{1,0:T(8,128)}), f32[64,4096]{1,0:T(8,128)}) %all-reduce.15.cloned.1.call-update) | async-done | bytes 1048592 | tf_op jit(solution)/shard_map/psum | solution.py:58
  568.7 9.3 %all-gather.3 = f32[512,64]{1,0:T(8,128)S(1)} all-gather(f32[64,64]{1,0:T(8,128)S(1)} %fusion.119), channel_id=5, replica_groups=mesh['blk'=8,'rows'=4] {'blk'}, dimensions={0}, use_global_device_ids=true | all-gather | bytes 147456 | tf_op jit(solution)/shard_map/all_gather | solution.py:31
  (109 shorter events, 137.6 us)
Async XLA Ops:
  6.5 2.8 copy-start
  6.5 123.8 %all-reduce.9.cloned.1.call-start = ((), (), s32[]{:S(2)}) async-start(), calls=%async_computation | async-start | bytes 2097152 | tf_op jit(solution)/shard_map/psum | solution.py:58
  12.5 10.4 %copy-start.5 = (s32[256,1]{0,1:T(1,128)S(1)}, s32[256,1]{0,1:T(1,128)}, u32[]{:S(2)}) copy-start(s32[256,1]{0,1:T(1,128)} %param.14) | copy-start | bytes 3076
  62.3 7.0 %copy-start.6 = (s32[256,1]{0,1:T(1,128)S(1)}, s32[256,1]{0,1:T(1,128)}, u32[]{:S(2)}) copy-start(s32[256,1]{0,1:T(1,128)} %param.15) | copy-start | bytes 3076
  78.7 196.9 %all-reduce.11.cloned.1.call-start = ((), (), s32[]{:S(2)}) async-start(), calls=%async_computation.1 | async-start | bytes 2097152 | tf_op jit(solution)/shard_map/psum | solution.py:58
  156.8 1.0 copy-start.2
  225.1 195.7 %all-reduce.13.cloned.1.call-start = ((), (), s32[]{:S(2)}) async-start(), calls=%async_computation.2 | async-start | bytes 2097152 | tf_op jit(solution)/shard_map/psum | solution.py:58
  302.1 1.0 copy-start.3
  370.4 195.5 %all-reduce.15.cloned.1.call-start = ((), (), s32[]{:S(2)}) async-start(), calls=%async_computation.3 | async-start | bytes 2097152 | tf_op jit(solution)/shard_map/psum | solution.py:58
  447.4 1.0 copy-start.4
  516.5 77.1 %copy-start.1 = (bf16[64,4096]{1,0:T(8,128)(2,1)S(1)}, bf16[64,4096]{1,0:T(8,128)(2,1)}, u32[]{:S(2)}) copy-start(bf16[64,4096]{1,0:T(8,128)(2,1)} %param.13) | copy-start | bytes 1572868
Sparse Core Ops, SparseCore 0:
  78.8 51.4 all-reduce.8
  225.3 50.2 all-reduce.10
  370.6 50.2 all-reduce.12
  515.6 50.2 all-reduce.14
